TPU v7x, 32 devices: a whole 2x2x4 slice. The times are simulated.
32 devices in a mesh: groups: 2 (over y), space: 8 (over z, x), section: 2 (over core).
Axes of the slice: x: 2, y: 2, z: 4, core: 2. Of those that a mesh axis runs over, the one named last changes fastest.
Arguments:
- atm_state: bfloat16 [4, 8, 256, 256], P(('groups', 'section'), 'space'), parts along dimension 0, may hold values from -6 to 6
- ocean_state: bfloat16 [4, 2048, 192], P(('groups', 'section'), 'space'), parts along dimension 0, may hold values from -6 to 6
- owners: int32 [8, 256, 2], P('space'), may hold values from 0 to 7, all different within a row; in each aligned block of 256 rows (0 to 255, 256 to 511, ..., all dimensions but the last counted through in order) at most 128 rows name the same one
- target_cell: int32 [8, 256, 2], P('space'), may hold values from 0 to 255
- margin_weight: float32 [8, 256, 2], P('space'), may hold values from 0.25 to 1
- sea_mask: int32 [8, 256], P('space'), may hold values 0 or 1
- conv_kernel: bfloat16 [9, 256, 256], replicated, may hold values from -0.125 to 0.125
- meridional_weight: bfloat16 [256, 256], replicated, may hold values from -0.375 to 0.375
- atm_gain: float32 [256], replicated, may hold values from 0.25 to 1.75
- atm_in: bfloat16 [256, 1024], replicated, may hold values from -0.375 to 0.375
- atm_out: bfloat16 [1024, 256], replicated, may hold values from -0.1875 to 0.1875
- flux_weight: bfloat16 [256, 128], replicated, may hold values from -0.375 to 0.375
- forcing_weight: bfloat16 [128, 192], replicated, may hold values from -0.5 to 0.5
- ocean_gain: float32 [192], replicated, may hold values from 0.25 to 1.75
- ocean_in: bfloat16 [192, 768], replicated, may hold values from -0.4375 to 0.4375
- ocean_out: bfloat16 [768, 192], replicated, may hold values from -0.21875 to 0.21875
- surface_weight: bfloat16 [192, 128], replicated, may hold values from -0.4375 to 0.4375
- feedback_weight: bfloat16 [128, 256], replicated, may hold values from -0.5 to 0.5
Outputs:
- atm_next: bfloat16 [4, 8, 256, 256], P(('groups', 'section'), 'space'), parts along dimension 0
- ocean_next: bfloat16 [4, 2048, 192], P(('groups', 'section'), 'space'), parts along dimension 0
There are 2 independent parts, one for each index of `groups`. A program takes and returns all parts, laid end to end along the dimension named above; an argument that names none is the same for every part. Nothing has to cross between parts.
Inputs may be any that keep to these rules, and one draw needn't show every extreme that they name: Within the 256 cells of one latitude band, no owner is named by more than 128 margin entries, a bound that some block reaches; the 2 owners of one cell differ.
All inputs are finite; a program needn't handle non-finite values. No bound on the sum of `sea_mask` on one device may be relied on, other than what follows from the above.
Results may differ from a plain program's by a relative error of at most 0.014.
Values may be sent and summed in bfloat16 or wider, within the bound.
A program may use at most 64 MiB of HBM per device.

v0:
```python
import math

import jax
import jax.numpy as jnp
from jax import lax
from jax.sharding import PartitionSpec as P


def extended(cells, sides, width):
    for axis, dim in sides:
        count = lax.axis_size(axis)
        ends = count - 1
        head = lax.slice_in_dim(cells, 0, width, axis=dim)
        tail = lax.slice_in_dim(cells, cells.shape[dim] - width, cells.shape[dim], axis=dim)
        cells = jnp.concatenate(
            [
                lax.ppermute(tail, axis, [(i, (i + 1) % count) for i in range(ends)]),
                cells,
                lax.ppermute(head, axis, [((i + 1) % count, i) for i in range(ends)]),
            ],
            axis=dim,
        )
    return cells


def entering(part, axis, combine, identity):
    place = lax.axis_index(axis)
    gathered = lax.all_gather(part, axis)
    state = jnp.zeros_like(part) + jnp.asarray(identity, part.dtype)

    def one(hop, state):
        return combine(state, lax.dynamic_index_in_dim(gathered, hop, 0, False))

    return lax.fori_loop(0, place, one, state)


def conv_taps(padded, kernel, lat_rows):
    channels = padded.shape[-1]
    columns = []
    for row_off in range(3):
        lat_band = padded[row_off : row_off + lat_rows]
        for col_off in range(3):
            columns.append(jnp.roll(lat_band, 1 - col_off, axis=1))
    stacked = jnp.concatenate(columns, axis=-1)
    flattened = stacked.reshape(-1, 9 * channels)
    result = jnp.dot(
        flattened, kernel.reshape(9 * channels, channels), preferred_element_type=jnp.float32
    )
    return result.reshape(lat_rows, padded.shape[1], channels)


def rms_scale(values, gain_vec):
    return values * lax.rsqrt(jnp.mean(values * values, axis=-1, keepdims=True) + 1e-06) * gain_vec


def add_terms(earlier, later):
    return earlier + later


def contract_first(left, right):
    return lax.dot_general(
        left, right, (((0,), (0,)), ((), ())), preferred_element_type=jnp.float32
    )


def local(
    atm_state,
    ocean_state,
    owners,
    target_cell,
    margin_weight,
    sea_mask,
    conv_kernel,
    meridional_weight,
    atm_gain,
    atm_in,
    atm_out,
    flux_weight,
    forcing_weight,
    ocean_gain,
    ocean_in,
    ocean_out,
    surface_weight,
    feedback_weight,
):
    atm_one = atm_state[0]
    ocn_one = ocean_state[0]
    lat_rows, lon_cells, channels = atm_one.shape
    margin_count = owners.shape[-1]
    flux_width = flux_weight.shape[1]
    peer_count = lax.axis_size("space")
    slot_count = max(2, 2 * lat_rows * lon_cells * margin_count // peer_count)
    lat_total = lat_rows * peer_count
    padded = extended(atm_one, (("space", 0),), 1)
    mixing = conv_taps(padded, conv_kernel, lat_rows)
    hidden = atm_one.astype(jnp.float32) + mixing
    zonal_sums = jnp.sum(hidden, axis=1) / math.sqrt(lon_cells)
    band_total = jnp.sum(zonal_sums, axis=0)
    before = entering(band_total, "space", add_terms, jnp.zeros_like(band_total))
    prefix = (before[None, :] + jnp.cumsum(zonal_sums, axis=0) - zonal_sums) / math.sqrt(lat_total)
    meridional = jnp.dot(
        prefix, meridional_weight.astype(jnp.float32), precision=lax.Precision.HIGHEST
    )
    lifted = (hidden + meridional[:, None, :]).reshape(-1, channels)
    normed = rms_scale(lifted, atm_gain).astype(jnp.bfloat16)
    activated = jax.nn.silu(jnp.dot(normed, atm_in, preferred_element_type=jnp.float32)).astype(
        jnp.bfloat16
    )
    atm_mid = (lifted + jnp.dot(activated, atm_out, preferred_element_type=jnp.float32)).astype(
        jnp.bfloat16
    )
    flux_rows = jnp.dot(atm_mid, flux_weight, preferred_element_type=jnp.float32)
    sea_cells = sea_mask.astype(jnp.float32).reshape(-1)
    weights = margin_weight.reshape(-1, margin_count)
    payload = (weights[:, :, None] * sea_cells[:, None, None] * flux_rows[:, None, :]).astype(
        jnp.bfloat16
    )
    payload = payload.reshape(-1, flux_width)
    owner_ids = owners.reshape(-1)
    owner_hits = (owner_ids[:, None] == jnp.arange(peer_count, dtype=jnp.int32)[None, :]).astype(
        jnp.int32
    )
    slot_rank = jnp.sum((jnp.cumsum(owner_hits, axis=0) - 1) * owner_hits, axis=1)
    slot_index = owner_ids * slot_count + slot_rank
    slot_total = peer_count * slot_count
    placement = slot_index[:, None] == jnp.arange(slot_total, dtype=jnp.int32)[None, :]
    place_bf = placement.astype(jnp.bfloat16)
    send_rows = contract_first(place_bf, payload).astype(jnp.bfloat16)
    entry_cells = target_cell.reshape(-1)
    send_cells = jnp.sum(placement.astype(jnp.int32) * entry_cells[:, None], axis=0)
    recv_rows, recv_cells = (
        lax.all_to_all(
            send_rows.reshape(peer_count, slot_count, flux_width),
            "space",
            split_axis=0,
            concat_axis=0,
            tiled=True,
        ),
        lax.all_to_all(
            send_cells.reshape(peer_count, slot_count),
            "space",
            split_axis=0,
            concat_axis=0,
            tiled=True,
        ),
    )
    recv_cells = recv_cells.reshape(-1)
    ocean_cells = ocn_one.shape[0]
    cell_onehot = (recv_cells[:, None] == jnp.arange(ocean_cells, dtype=jnp.int32)[None, :]).astype(
        jnp.bfloat16
    )
    forcing = contract_first(cell_onehot, recv_rows.reshape(-1, flux_width)).astype(jnp.bfloat16)
    ocean_lift = ocn_one.astype(jnp.float32) + jnp.dot(
        forcing, forcing_weight, preferred_element_type=jnp.float32
    )
    ocean_normed = rms_scale(ocean_lift, ocean_gain).astype(jnp.bfloat16)
    ocean_act = jax.nn.silu(
        jnp.dot(ocean_normed, ocean_in, preferred_element_type=jnp.float32)
    ).astype(jnp.bfloat16)
    ocean_new = (
        ocean_lift + jnp.dot(ocean_act, ocean_out, preferred_element_type=jnp.float32)
    ).astype(jnp.bfloat16)
    surface = jnp.dot(ocean_new, surface_weight, preferred_element_type=jnp.float32).astype(
        jnp.bfloat16
    )
    back_rows = jnp.dot(cell_onehot, surface, preferred_element_type=jnp.float32).astype(
        jnp.bfloat16
    )
    returned = lax.all_to_all(
        back_rows.reshape(peer_count, slot_count, flux_width),
        "space",
        split_axis=0,
        concat_axis=0,
        tiled=True,
    )
    picked = jnp.dot(place_bf, returned.reshape(-1, flux_width), preferred_element_type=jnp.float32)
    picked = picked.reshape(-1, margin_count, flux_width)
    feedback = jnp.sum(weights[:, :, None] * picked, axis=1).astype(jnp.bfloat16)
    back_term = jnp.dot(feedback, feedback_weight, preferred_element_type=jnp.float32)
    atm_new = (atm_mid.astype(jnp.float32) + sea_cells[:, None] * back_term).astype(jnp.bfloat16)
    return (atm_new.reshape(1, lat_rows, lon_cells, channels), ocean_new[None])


def solution(mesh):
    placed = (
        P(("groups", "section"), "space", None, None),
        P(("groups", "section"), "space", None),
        P("space", None, None),
        P("space", None, None),
        P("space", None, None),
        P("space", None),
        P(),
        P(),
        P(),
        P(),
        P(),
        P(),
        P(),
        P(),
        P(),
        P(),
        P(),
        P(),
    )
    return jax.shard_map(
        local,
        mesh=mesh,
        in_specs=placed,
        out_specs=(
            P(("groups", "section"), "space", None, None),
            P(("groups", "section"), "space", None),
        ),
        check_vma=False,
    )
```

profile of v0, /device:TPU:0, one launch (start us, length us, event | category | flops | bytes accessed | tf_op | source)
XLA Modules:
  0.0 71.0 jit_solution(671286517310417763)
XLA Ops:
  0.7 5.0 %collective-permute-start = (bf16[1,256,256]{2,1,0:T(8,128)(2,1)}, bf16[1,256,256]{2,1,0:T(8,128)(2,1)S(1)}, u32[]{:S(2)}, u32[]{:S(2)}) collective-permute-start(bf16[1,256,256]{2,1,0:T(8,128)(2,1)} %bitcast.71), channel_id=1, source_target_pairs={{0,2},{2,4},{4,6},{6,8},{8,10},{10,12},{12,14},{1,3},{3,5},{5,7},{... | collective-permute-start | bytes 393224 | tf_op jit(solution)/shard_map/ppermute | solution.py:17
  5.7 1.3 %collective-permute-start.1 = (bf16[1,256,256]{2,1,0:T(8,128)(2,1)}, bf16[1,256,256]{2,1,0:T(8,128)(2,1)S(1)}, u32[]{:S(2)}, u32[]{:S(2)}) collective-permute-start(bf16[1,256,256]{2,1,0:T(8,128)(2,1)} %bitcast.72), channel_id=1, source_target_pairs={{2,0},{4,2},{6,4},{8,6},{10,8},{12,10},{14,12},{3,1},{5,3},{7,5},{... | collective-permute-start | bytes 393224 | tf_op jit(solution)/shard_map/ppermute | solution.py:19
  7.0 0.8 %copy.35 = s32[1,256,2]{2,1,0:T(8,128)S(1)} copy(s32[1,256,2]{1,2,0:T(2,128)} %param.22) | data formatting | bytes 4096 | tf_op args[2]
  7.8 0.1 eq.79
  8.0 0.1 eq.75
  8.1 1.1 %reduce-window.6 = s32[8,4,128]{2,0,1:T(8,128)S(1)} reduce-window(s32[8,4,128]{2,0,1:T(8,128)S(1)} %fusion.41, s32[]{:T(128)} %constant.39.clone.1), window={size=1x1x128 pad=0_0x0_0x127_0}, to_apply=%region_4.5 | reduce-window | flops 520192 | bytes 32772 | tf_op jit(solution)/shard_map/reduce-window
  9.3 0.2 slice_reduce_fusion
  9.6 0.8 %copy.39 = s32[1,256,2]{2,1,0:T(8,128)S(1)} copy(s32[1,256,2]{1,2,0:T(2,128)} %param.23) | data formatting | bytes 4096 | tf_op args[3]
  10.4 0.1 mul.144
  10.6 0.9 %select_reduce_fusion = s32[1024]{0:T(1024)} fusion(s32[512]{0:T(512)S(1)} %mul.144, s32[512]{0:T(512)S(1)} %multiply_add_fusion), kind=kLoop, calls=%fused_computation.1 | loop fusion | flops 1571840 | bytes 8192 | tf_op jit(solution)/shard_map/reduce_sum | solution.py:130
  11.5 7.0 %all-to-all-start = ((s32[8,1,128]{2,1,0:T(1,128)}), s32[8,1,128]{2,1,0:T(1,128)S(1)}, u32[]{:S(2)}, u32[]{:S(2)}) async-start(s32[8,1,128]{2,1,0:T(1,128)} %bitcast.14), calls=%async_computation | async-start | bytes 8192 | tf_op jit(solution)/shard_map/all_to_all | solution.py:139
  18.4 1.0 %fusion.47 = (bf16[1,255,256]{2,1,0:T(8,128)(2,1)S(1)}, bf16[1,255,256]{2,1,0:T(8,128)(2,1)S(1)}) fusion(bf16[1,256,256]{2,1,0:T(8,128)(2,1)} %bitcast.73), kind=kLoop, calls=%fused_computation.73 | loop fusion | bytes 522240 | tf_op jit(solution)/shard_map/jit(_roll_static)/slice | solution.py:43
  19.6 0.1 mul.148
  19.7 0.1 copy.40
  19.9 0.1 broadcast_in_dim_reshape.2
  20.5 0.5 fusion.51
  21.0 21.0 %all-gather.1 = f32[8,1,256]{2,1,0:T(1,128)S(1)} all-gather(f32[1,1,256]{2,1,0:T(1,128)S(1)} %bitcast.86), channel_id=2, replica_groups=mesh['groups'=2,'space'=8,'section'=2] {'space'}, dimensions={0}, use_global_device_ids=true | all-gather | bytes 9216 | tf_op jit(solution)/shard_map/all_gather | solution.py:28
  42.0 0.1 fusion.52
  42.2 0.2 multiply_reduce_fusion
  42.4 0.6 fusion.18
  43.0 0.2 copy-done.3
  43.2 0.2 fusion.53
  43.5 0.9 %fusion.4 = bf16[1024,128]{1,0:T(8,128)(2,1)S(1)} fusion(s32[512]{0:T(512)S(1)} %multiply_add_fusion, f32[512,128]{1,0:T(8,128)S(1)} %bitcast.75, f32[512]{0:T(512)S(1)} %mul.149), kind=kOutput, calls=%fused_computation.7 | convolution fusion | flops 135004160 | bytes 528384 | tf_op jit(solution)/shard_map/dot_general | solution.py:61
  44.4 10.6 %all_to_all.19 = bf16[8,128,128]{2,1,0:T(8,128)(2,1)S(1)} all-to-all(bf16[8,128,128]{2,1,0:T(8,128)(2,1)S(1)} %bitcast.77), channel_id=1, replica_groups=mesh['groups'=2,'space'=8,'section'=2] {'space'}, dimensions={0} | all-to-all | bytes 524288 | tf_op jit(solution)/shard_map/all_to_all | solution.py:132
  55.1 0.8 %multiply_reduce_fusion.1 = (f32[256]{0:T(256)S(1)}, f32[256,192]{0,1:T(8,128)S(1)}) fusion(bf16[128,192]{0,1:T(8,128)(2,1)S(1)} %copy-done.12, bf16[1024,128]{1,0:T(8,128)(2,1)S(1)} %bitcast.78, s32[1024]{0:T(1024)S(1)} %bitcast.87, bf16[1,256,192]{1,2,0:T(8,128)(2,1)S(1)} %copy-done.11), kind=kOutput, calls=%fused_computation.37 | convolution fusion | flops 80183040 | bytes 611328 | tf_op jit(solution)/shard_map/dot_general | solution.py:153
  55.9 0.7 fusion.19
  56.7 1.2 %convolution_convert_fusion = bf16[1024,128]{1,0:T(8,128)(2,1)} fusion(bf16[256,192]{0,1:T(8,128)(2,1)S(1)} %fusion.19, bf16[192,128]{1,0:T(8,128)(2,1)S(1)} %copy-done.13, s32[1024]{0:T(1024)S(1)} %bitcast.88), kind=kOutput, calls=%fused_computation.8 | convolution fusion | flops 80117760 | bytes 413696 | tf_op jit(solution)/shard_map/dot_general | solution.py:166
  58.0 3.5 %all-to-all-start.2 = ((bf16[8,128,128]{2,1,0:T(8,128)(2,1)}), bf16[8,128,128]{2,1,0:T(8,128)(2,1)S(1)}, u32[]{:S(2)}, u32[]{:S(2)}) async-start(bf16[8,128,128]{2,1,0:T(8,128)(2,1)} %bitcast.20), calls=%async_computation.2 | async-start | bytes 524288 | tf_op jit(solution)/shard_map/all_to_all | solution.py:169
  61.5 0.1 reduce_sum.63
  61.8 7.9 %all-to-all-done.2 = bf16[8,128,128]{2,1,0:T(8,128)(2,1)S(1)} async-done(((bf16[8,128,128]{2,1,0:T(8,128)(2,1)}), bf16[8,128,128]{2,1,0:T(8,128)(2,1)S(1)}, u32[]{:S(2)}, u32[]{:S(2)}) %all-to-all-start.2) | async-done | bytes 262176 | tf_op jit(solution)/shard_map/all_to_all | solution.py:169
  69.7 0.5 fusion.15
  70.2 0.8 %fusion.20 = bf16[1,1,256,256]{3,2,1,0:T(8,128)(2,1)} fusion(bf16[128,256]{1,0:T(8,128)(2,1)S(1)} %copy-done.4, bf16[256,256]{1,0:T(8,128)(2,1)S(1)} %fusion.18, f32[256]{0:T(256)S(1)} %bitcast.82, bf16[256,128]{1,0:T(8,128)(2,1)S(1)} %fusion.15), kind=kOutput, calls=%fused_computation.22 | convolution fusion | flops 17039360 | bytes 394240 | tf_op jit(solution)/shard_map/dot_general | solution.py:179
  (68 shorter events, 0.9 us)
Async XLA Ops:
  0.6 19.8 %copy-start = (bf16[9,256,256]{2,1,0:T(8,128)(2,1)S(1)}, bf16[9,256,256]{2,1,0:T(8,128)(2,1)}, u32[]{:S(2)}) copy-start(bf16[9,256,256]{2,1,0:T(8,128)(2,1)} %param.26) | copy-start | bytes 3538948
  0.6 19.4 %copy-start.1 = (bf16[1,1,256,256]{3,2,1,0:T(8,128)(2,1)S(1)}, bf16[1,1,256,256]{3,2,1,0:T(8,128)(2,1)}, u32[]{:S(2)}) copy-start(bf16[1,1,256,256]{3,2,1,0:T(8,128)(2,1)} %param.20) | copy-start | bytes 393220
  0.7 18.8 %copy-start.6 = (s32[1,256]{1,0:T(1,128)S(1)}, s32[1,256]{1,0:T(1,128)}, u32[]{:S(2)}) copy-start(s32[1,256]{1,0:T(1,128)} %param.25) | copy-start | bytes 3076
  0.7 19.1 %copy-start.5 = (f32[1,256,2]{1,2,0:T(2,128)S(1)}, f32[1,256,2]{1,2,0:T(2,128)}, u32[]{:S(2)}) copy-start(f32[1,256,2]{1,2,0:T(2,128)} %param.24) | copy-start | bytes 6148
  0.7 19.4 %collective-permute-start = (bf16[1,256,256]{2,1,0:T(8,128)(2,1)}, bf16[1,256,256]{2,1,0:T(8,128)(2,1)S(1)}, u32[]{:S(2)}, u32[]{:S(2)}) collective-permute-start(bf16[1,256,256]{2,1,0:T(8,128)(2,1)} %bitcast.71), channel_id=1, source_target_pairs={{0,2},{2,4},{4,6},{6,8},{8,10},{10,12},{12,14},{1,3},{3,5},{5,7},{... | collective-permute-start | bytes 393224 | tf_op jit(solution)/shard_map/ppermute | solution.py:17
  5.7 14.6 %collective-permute-start.1 = (bf16[1,256,256]{2,1,0:T(8,128)(2,1)}, bf16[1,256,256]{2,1,0:T(8,128)(2,1)S(1)}, u32[]{:S(2)}, u32[]{:S(2)}) collective-permute-start(bf16[1,256,256]{2,1,0:T(8,128)(2,1)} %bitcast.72), channel_id=1, source_target_pairs={{2,0},{4,2},{6,4},{8,6},{10,8},{12,10},{14,12},{3,1},{5,3},{7,5},{... | collective-permute-start | bytes 393224 | tf_op jit(solution)/shard_map/ppermute | solution.py:19
  11.5 32.9 %all-to-all-start = ((s32[8,1,128]{2,1,0:T(1,128)}), s32[8,1,128]{2,1,0:T(1,128)S(1)}, u32[]{:S(2)}, u32[]{:S(2)}) async-start(s32[8,1,128]{2,1,0:T(1,128)} %bitcast.14), calls=%async_computation | async-start | bytes 8192 | tf_op jit(solution)/shard_map/all_to_all | solution.py:139
  20.4 21.6 %copy-start.2 = (bf16[256,256]{1,0:T(8,128)(2,1)S(1)}, bf16[256,256]{1,0:T(8,128)(2,1)}, u32[]{:S(2)}) copy-start(bf16[256,256]{1,0:T(8,128)(2,1)} %param.27) | copy-start | bytes 393220
  20.5 21.9 %copy-start.7 = (bf16[1024,256]{1,0:T(8,128)(2,1)S(1)}, bf16[1024,256]{1,0:T(8,128)(2,1)}, u32[]{:S(2)}) copy-start(bf16[1024,256]{1,0:T(8,128)(2,1)} %param.30) | copy-start | bytes 1572868
  20.5 21.9 %copy-start.8 = (bf16[256,1024]{1,0:T(8,128)(2,1)S(1)}, bf16[256,1024]{1,0:T(8,128)(2,1)}, u32[]{:S(2)}) copy-start(bf16[256,1024]{1,0:T(8,128)(2,1)} %param.29) | copy-start | bytes 1572868
  20.5 21.9 %copy-start.14 = (f32[256]{0:T(256)S(1)}, f32[256]{0:T(256)}, u32[]{:S(2)}) copy-start(f32[256]{0:T(256)} %param.28) | copy-start | bytes 3076
  42.4 0.8 %copy-start.3 = (bf16[256,128]{1,0:T(8,128)(2,1)S(1)}, bf16[256,128]{1,0:T(8,128)(2,1)}, u32[]{:S(2)}) copy-start(bf16[256,128]{1,0:T(8,128)(2,1)} %param.31) | copy-start | bytes 196612
  43.2 11.9 %copy-start.11 = (bf16[1,256,192]{1,2,0:T(8,128)(2,1)S(1)}, bf16[1,256,192]{1,2,0:T(8,128)(2,1)}, u32[]{:S(2)}) copy-start(bf16[1,256,192]{1,2,0:T(8,128)(2,1)} %param.21) | copy-start | bytes 294916
  43.2 11.9 %copy-start.12 = (bf16[128,192]{0,1:T(8,128)(2,1)S(1)}, bf16[128,192]{0,1:T(8,128)(2,1)}, u32[]{:S(2)}) copy-start(bf16[128,192]{0,1:T(8,128)(2,1)} %param.32) | copy-start | bytes 147460
  43.5 12.4 %copy-start.9 = (bf16[768,192]{0,1:T(8,128)(2,1)S(1)}, bf16[768,192]{0,1:T(8,128)(2,1)}, u32[]{:S(2)}) copy-start(bf16[768,192]{0,1:T(8,128)(2,1)} %param.35) | copy-start | bytes 884740
  43.5 12.4 %copy-start.10 = (bf16[192,768]{1,0:T(8,128)(2,1)S(1)}, bf16[192,768]{1,0:T(8,128)(2,1)}, u32[]{:S(2)}) copy-start(bf16[192,768]{1,0:T(8,128)(2,1)} %param.34) | copy-start | bytes 884740
  43.5 12.4 %copy-start.15 = (f32[192]{0:T(256)S(1)}, f32[192]{0:T(256)}, u32[]{:S(2)}) copy-start(f32[192]{0:T(256)} %param.33) | copy-start | bytes 2308
  55.9 0.8 %copy-start.13 = (bf16[192,128]{1,0:T(8,128)(2,1)S(1)}, bf16[192,128]{1,0:T(8,128)(2,1)}, u32[]{:S(2)}) copy-start(bf16[192,128]{1,0:T(8,128)(2,1)} %param.36) | copy-start | bytes 147460
  56.7 13.5 %copy-start.16 = (bf16[256,192]{0,1:T(8,128)(2,1)}, bf16[256,192]{0,1:T(8,128)(2,1)S(1)}, u32[]{:S(2)}) copy-start(bf16[256,192]{0,1:T(8,128)(2,1)S(1)} %fusion.19) | copy-start | bytes 294916
  58.0 12.2 %copy-start.4 = (bf16[128,256]{1,0:T(8,128)(2,1)S(1)}, bf16[128,256]{1,0:T(8,128)(2,1)}, u32[]{:S(2)}) copy-start(bf16[128,256]{1,0:T(8,128)(2,1)} %param.37) | copy-start | bytes 196612
  58.0 11.7 %all-to-all-start.2 = ((bf16[8,128,128]{2,1,0:T(8,128)(2,1)}), bf16[8,128,128]{2,1,0:T(8,128)(2,1)S(1)}, u32[]{:S(2)}, u32[]{:S(2)}) async-start(bf16[8,128,128]{2,1,0:T(8,128)(2,1)} %bitcast.20), calls=%async_computation.2 | async-start | bytes 524288 | tf_op jit(solution)/shard_map/all_to_all | solution.py:169
where the time goes:
time: 71.6 us; the launch traced here: 71 us
  blocking collectives  31.6 us (44%)
  starting transfers between devices  16.8 us (23%)
  waiting for transfers between devices  7.92 us (11%)
  matrix products  6.33 us (9%)
  local copies, waits for them, and re-layouts  4.64 us (6%)
  other arithmetic  2.53 us (4%)
  between operations  1.17 us (2%)
    all_gather x1, blocking collectives, entering(): gathered = lax.all_gather(part, axis)  21 us
    all_to_all x1, blocking collectives, local(): lax.all_to_all(send_rows.reshape(peer_count, slot_count, flux_width), 'sp...  10.6 us
    all_to_all x1, waiting for transfers between devices, local(): lax.all_to_all(back_rows.reshape(peer_count, slot_count, flux_width), 'sp...  7.91 us
    all_to_all x1, starting transfers between devices, local(): lax.all_to_all(send_cells.reshape(peer_count, slot_count), 'space', split...  6.96 us
    ppermute x1, starting transfers between devices, extended(): lax.ppermute(tail, axis, [(i, (i + 1) % count) for i in range(ends)])  5.01 us
    all_to_all x1, starting transfers between devices, local(): lax.all_to_all(back_rows.reshape(peer_count, slot_count, flux_width), 'sp...  3.54 us
    unnamed x41, local copies, waits for them, and re-layouts  2.22 us
  transfers between devices with their start and end apart: 4, of which 1 were waited for; matrix products, arithmetic and copies ran while one was open for 13% of the time, Pallas kernels for 0%

commit v1 on v0

v1 whole, which is shorter than its diff:
```python
import functools
import math

import jax
import jax.numpy as jnp
from jax import lax
from jax.experimental import pallas as pl
from jax.experimental.pallas import tpu as pltpu
from jax.sharding import PartitionSpec as P

F32 = jnp.float32
BF16 = jnp.bfloat16


def mm(left, right):
    return jnp.dot(left, right, preferred_element_type=F32)


def mm_nt(left, right):
    return lax.dot_general(left, right, (((1,), (1,)), ((), ())), preferred_element_type=F32)


def rms_scale(values, gain_vec):
    return values * lax.rsqrt(jnp.mean(values * values, axis=-1, keepdims=True) + 1e-06) * gain_vec


def silu(values):
    return values / (1.0 + jnp.exp(-values))


def thirds(rows):
    high = rows.astype(BF16).astype(F32)
    rest = rows - high
    middle = rest.astype(BF16).astype(F32)
    low = rest - middle
    row = lax.broadcasted_iota(jnp.int32, rows.shape, 0)
    return jnp.where(
        row == 0, high, jnp.where(row == 1, middle, jnp.where(row == 2, low, 0.0))
    ).astype(BF16)


def each(count, body):
    if count <= 8:
        for step in range(count):
            body(step)
    else:
        lax.fori_loop(0, count, lambda step, carry: (body(step), carry)[1], 0)


def kernel(
    n,
    slots,
    atm_ref,
    own_ref,
    tgt_ref,
    wgt_ref,
    sea_ref,
    again_ref,
    ogain_ref,
    ocn_hbm,
    conv_hbm,
    mer_hbm,
    ain_hbm,
    aout_hbm,
    flux_hbm,
    forc_hbm,
    oin_hbm,
    oout_hbm,
    surf_hbm,
    feed_hbm,
    atm_out_ref,
    ocn_out_ref,
    ocn_v,
    conv_v,
    mer_v,
    ain_v,
    aout_v,
    flux_v,
    forc_v,
    oin_v,
    oout_v,
    surf_v,
    feed_v,
    north,
    south,
    sums_send,
    sums_all,
    cells_send,
    cells_all,
    pack,
    unpack,
    gather_t,
    gather,
    send_rows,
    recv_rows,
    back_rows,
    ret_rows,
    mid_v,
    ocn_new,
    load_sem,
    out_sem,
    halo_send,
    halo_recv,
    sum_send_sem,
    sum_recv_sem,
    cell_send_sem,
    cell_recv_sem,
    flux_send_sem,
    flux_recv_sem,
    back_send_sem,
    back_recv_sem,
):
    me = lax.axis_index("space")
    lon, channels = atm_ref.shape
    barrier = pltpu.get_barrier_semaphore()
    for d in range(1, n):
        pl.semaphore_signal(
            barrier,
            inc=1,
            device_id={"space": lax.rem(me + d, n)},
            device_id_type=pl.DeviceIdType.MESH,
        )

    loads = [
        pltpu.make_async_copy(src, dst, load_sem.at[i])
        for i, (src, dst) in enumerate(
            [
                (conv_hbm, conv_v),
                (mer_hbm, mer_v),
                (ain_hbm, ain_v),
                (aout_hbm, aout_v),
                (flux_hbm, flux_v),
                (ocn_hbm, ocn_v),
                (forc_hbm, forc_v),
                (oin_hbm, oin_v),
                (oout_hbm, oout_v),
                (surf_hbm, surf_v),
                (feed_hbm, feed_v),
            ]
        )
    ]
    for load in loads:
        load.start()

    def remote(src, dst, send_sem, recv_sem, peer):
        return pltpu.make_async_remote_copy(
            src_ref=src,
            dst_ref=dst,
            send_sem=send_sem,
            recv_sem=recv_sem,
            device_id={"space": peer},
            device_id_type=pl.DeviceIdType.MESH,
        )

    total = jnp.sum(atm_ref[...].astype(F32), axis=0, keepdims=True)
    sums_send[...] = jnp.broadcast_to(total, sums_send.shape)
    sums_all[me] = jnp.broadcast_to(total, sums_send.shape)

    own_row = jnp.concatenate([own_ref[0:1, :], own_ref[1:2, :]], axis=1)
    entries = own_row.shape[1]
    hits = own_row == lax.broadcasted_iota(jnp.int32, (n, entries), 0)
    earlier = lax.broadcasted_iota(jnp.int32, (entries, entries), 0) < lax.broadcasted_iota(
        jnp.int32, (entries, entries), 1
    )
    counts = mm(hits.astype(F32).astype(BF16), earlier.astype(F32).astype(BF16))
    rank = jnp.sum(jnp.where(hits, counts, 0.0), axis=0, keepdims=True)
    slot_row = own_row.astype(F32) * float(slots) + rank
    sea_row = sea_ref[...].astype(F32)
    slot0, slot1 = slot_row[:, :lon], slot_row[:, lon:]
    weight0 = wgt_ref[0:1, :] * sea_row
    weight1 = wgt_ref[1:2, :] * sea_row
    target = tgt_ref[...].astype(F32)
    target0 = jnp.broadcast_to(target[0:1, :], (8, lon)).astype(BF16)
    target1 = jnp.broadcast_to(target[1:2, :], (8, lon)).astype(BF16)

    def pack_one(p):
        place = (lax.broadcasted_iota(jnp.int32, (slots, lon), 0) + p * slots).astype(F32)
        hit0, hit1 = slot0 == place, slot1 == place
        pack[p] = (jnp.where(hit0, weight0, 0.0) + jnp.where(hit1, weight1, 0.0)).astype(BF16)
        cells_send[p] = mm_nt(target0, jnp.where(hit0, 1.0, 0.0).astype(BF16)) + mm_nt(
            target1, jnp.where(hit1, 1.0, 0.0).astype(BF16)
        )

    each(n, pack_one)
    cells_all[me] = cells_send[me]

    pl.semaphore_wait(barrier, n - 1)

    up = remote(atm_ref, north, halo_send.at[0], halo_recv.at[0], lax.rem(me + 1, n))
    down = remote(atm_ref, south, halo_send.at[1], halo_recv.at[1], lax.rem(me + n - 1, n))

    sum_copies, cell_copies = [], []
    for d in range(1, n):
        peer = lax.rem(me + d, n)
        sum_copies.append(
            remote(sums_send, sums_all.at[me], sum_send_sem.at[d], sum_recv_sem.at[d], peer)
        )
        sum_copies[-1].start()

    @pl.when(me < n - 1)
    def _():
        up.start()

    @pl.when(me > 0)
    def _():
        down.start()

    for d in range(1, n):
        peer = lax.rem(me + d, n)
        cell_copies.append(
            remote(
                cells_send.at[peer],
                cells_all.at[me],
                cell_send_sem.at[d],
                cell_recv_sem.at[d],
                peer,
            )
        )
        cell_copies[-1].start()

    @pl.when(me == 0)
    def _():
        north[...] = jnp.zeros_like(north)

    @pl.when(me == n - 1)
    def _():
        south[...] = jnp.zeros_like(south)

    stacked = jnp.concatenate(
        [slot0, slot1, weight0, weight1, jnp.zeros((4, lon), F32)], axis=0
    )
    columns = jnp.transpose(stacked)
    slot0c, slot1c = columns[:, 0:1], columns[:, 1:2]
    weight0c, weight1c = columns[:, 2:3], columns[:, 3:4]

    def unpack_one(p):
        place = (lax.broadcasted_iota(jnp.int32, (lon, slots), 1) + p * slots).astype(F32)
        unpack[:, pl.ds(p * slots, slots)] = (
            jnp.where(slot0c == place, weight0c, 0.0) + jnp.where(slot1c == place, weight1c, 0.0)
        ).astype(BF16)

    each(n, unpack_one)

    loads[0].wait()
    centre = atm_ref[...]
    taps = [mm(centre, conv_v[3 + b]) for b in range(3)]

    for copy in sum_copies:
        copy.wait_recv()
    zeros = jnp.zeros((8, channels), F32)

    def tally(p, sums):
        before, through, after = sums
        row = sums_all[p]
        before = before + jnp.where(p < me - 1, row, 0.0)
        through = through + jnp.where(p < me, row, 0.0)
        after = after + jnp.where((p >= 1) & (p <= me), row, 0.0)
        return before, through, after

    if n <= 8:
        carried = (zeros, zeros, zeros)
        for p in range(n):
            carried = tally(p, carried)
    else:
        carried = lax.fori_loop(0, n, tally, (zeros, zeros, zeros))
    mixed = jnp.zeros((8, channels), F32)
    for a in range(3):
        parts = thirds(carried[a])
        for b in range(3):
            mixed = mixed + mm(parts, conv_v[3 * a + b])
    prefix = (carried[1][0:1, :] + jnp.sum(mixed, axis=0, keepdims=True)) * (
        1.0 / (math.sqrt(lon) * math.sqrt(n))
    )
    loads[1].wait()
    meridional = jnp.sum(
        mm(thirds(jnp.broadcast_to(prefix, (8, channels))), mer_v[...]), axis=0, keepdims=True
    )

    for copy in cell_copies:
        copy.wait_recv()
    cells = ocn_v.shape[0]

    def gather_one(p):
        named = cells_all[p]
        rows = lax.broadcasted_iota(jnp.int32, (cells, slots), 0).astype(F32)
        gather_t[:, pl.ds(p * slots, slots)] = jnp.where(named[0:1, :] == rows, 1.0, 0.0).astype(
            BF16
        )
        lanes = lax.broadcasted_iota(jnp.int32, (slots, cells), 1).astype(F32)
        gather[p] = jnp.where(jnp.transpose(named)[:, 0:1] == lanes, 1.0, 0.0).astype(BF16)

    each(n, gather_one)

    for load in loads[2:]:
        load.wait()

    @pl.when(me > 0)
    def _():
        up.wait_recv()

    @pl.when(me < n - 1)
    def _():
        down.wait_recv()

    above, below = north[...], south[...]
    taps = [taps[b] + mm(above, conv_v[b]) + mm(below, conv_v[6 + b]) for b in range(3)]
    mixing = pltpu.roll(taps[0], 1, 0) + taps[1] + pltpu.roll(taps[2], lon - 1, 0)
    lifted = atm_ref[...].astype(F32) + mixing + meridional
    normed = rms_scale(lifted, again_ref[...]).astype(BF16)
    activated = silu(mm(normed, ain_v[...])).astype(BF16)
    atm_mid = (lifted + mm(activated, aout_v[...])).astype(BF16)
    mid_v[...] = atm_mid
    flux = mm(atm_mid, flux_v[...]).astype(BF16)

    flux_copies = []
    for d in range(1, n):
        peer = lax.rem(me + d, n)
        send_rows[peer] = mm(pack[peer], flux).astype(BF16)
        flux_copies.append(
            remote(
                send_rows.at[peer],
                recv_rows.at[me],
                flux_send_sem.at[d],
                flux_recv_sem.at[d],
                peer,
            )
        )
        flux_copies[-1].start()
    recv_rows[me] = mm(pack[me], flux).astype(BF16)
    for copy in flux_copies:
        copy.wait_recv()

    width = flux.shape[1]
    block = math.gcd(n, 8)

    def reduced(matrix, rows):
        def term(q, acc):
            part = rows[pl.ds(q * block, block)].reshape(block * slots, width)
            return acc + mm(matrix[:, pl.ds(q * block * slots, block * slots)], part)

        acc = jnp.zeros((matrix.shape[0], width), F32)
        if n == block:
            return term(0, acc)
        return lax.fori_loop(0, n // block, term, acc)

    forcing = reduced(gather_t, recv_rows).astype(BF16)
    ocean_lift = ocn_v[...].astype(F32) + mm(forcing, forc_v[...])
    ocean_normed = rms_scale(ocean_lift, ogain_ref[...]).astype(BF16)
    ocean_act = silu(mm(ocean_normed, oin_v[...])).astype(BF16)
    ocean_next = (ocean_lift + mm(ocean_act, oout_v[...])).astype(BF16)
    surface = mm(ocean_next, surf_v[...]).astype(BF16)

    back_copies = []
    for d in range(1, n):
        peer = lax.rem(me + d, n)
        back_rows[peer] = mm(gather[peer], surface).astype(BF16)
        back_copies.append(
            remote(
                back_rows.at[peer],
                ret_rows.at[me],
                back_send_sem.at[d],
                back_recv_sem.at[d],
                peer,
            )
        )
        back_copies[-1].start()
    ret_rows[me] = mm(gather[me], surface).astype(BF16)
    ocn_new[...] = ocean_next
    put = pltpu.make_async_copy(ocn_new, ocn_out_ref, out_sem)
    put.start()

    for copies in (sum_copies, cell_copies, flux_copies):
        for copy in copies:
            copy.wait_send()

    @pl.when(me < n - 1)
    def _():
        up.wait_send()

    @pl.when(me > 0)
    def _():
        down.wait_send()

    for copy in back_copies:
        copy.wait_recv()
    feedback = reduced(unpack, ret_rows).astype(BF16)
    atm_out_ref[...] = (mid_v[...].astype(F32) + mm(feedback, feed_v[...])).astype(BF16)
    for copy in back_copies:
        copy.wait_send()
    put.wait()


def local(
    atm_state,
    ocean_state,
    owners,
    target_cell,
    margin_weight,
    sea_mask,
    conv_kernel,
    meridional_weight,
    atm_gain,
    atm_in,
    atm_out,
    flux_weight,
    forcing_weight,
    ocean_gain,
    ocean_in,
    ocean_out,
    surface_weight,
    feedback_weight,
):
    _, lat_rows, lon, channels = atm_state.shape
    cells, ocn_ch = ocean_state.shape[1:]
    margins = owners.shape[-1]
    width = flux_weight.shape[1]
    n = lax.axis_size("space")
    assert lat_rows == 1 and margins == 2 and cells <= 256
    slots = max(2, 2 * lon * margins // n)
    slots = -(-slots // 128) * 128
    vmem = pl.BlockSpec(memory_space=pltpu.VMEM)
    hbm = pl.BlockSpec(memory_space=pl.ANY)
    weights = [
        ocean_state[0],
        conv_kernel,
        meridional_weight,
        atm_in,
        atm_out,
        flux_weight,
        forcing_weight,
        ocean_in,
        ocean_out,
        surface_weight,
        feedback_weight,
    ]
    dma = lambda count: pltpu.SemaphoreType.DMA((count,))
    atm_new, ocn_new = pl.pallas_call(
        functools.partial(kernel, n, slots),
        out_shape=(
            jax.ShapeDtypeStruct((lon, channels), BF16),
            jax.ShapeDtypeStruct((cells, ocn_ch), BF16),
        ),
        in_specs=[vmem] * 7 + [hbm] * len(weights),
        out_specs=(vmem, hbm),
        scratch_shapes=[pltpu.VMEM(w.shape, w.dtype) for w in weights]
        + [
            pltpu.VMEM((lon, channels), BF16),
            pltpu.VMEM((lon, channels), BF16),
            pltpu.VMEM((8, channels), F32),
            pltpu.VMEM((n, 8, channels), F32),
            pltpu.VMEM((n, 8, slots), F32),
            pltpu.VMEM((n, 8, slots), F32),
            pltpu.VMEM((n, slots, lon), BF16),
            pltpu.VMEM((lon, n * slots), BF16),
            pltpu.VMEM((cells, n * slots), BF16),
            pltpu.VMEM((n, slots, cells), BF16),
            pltpu.VMEM((n, slots, width), BF16),
            pltpu.VMEM((n, slots, width), BF16),
            pltpu.VMEM((n, slots, width), BF16),
            pltpu.VMEM((n, slots, width), BF16),
            pltpu.VMEM((lon, channels), BF16),
            pltpu.VMEM((cells, ocn_ch), BF16),
            dma(len(weights)),
            pltpu.SemaphoreType.DMA,
            dma(2),
            dma(2),
        ]
        + [dma(n)] * 8,
        compiler_params=pltpu.CompilerParams(
            collective_id=0, has_side_effects=True, vmem_limit_bytes=62 * 1024 * 1024
        ),
    )(
        atm_state.reshape(lon, channels),
        jnp.swapaxes(owners[0], 0, 1),
        jnp.swapaxes(target_cell[0], 0, 1),
        jnp.swapaxes(margin_weight[0], 0, 1),
        sea_mask,
        atm_gain[None, :],
        ocean_gain[None, :],
        *weights,
    )
    return atm_new.reshape(1, lat_rows, lon, channels), ocn_new[None]


def solution(mesh):
    state = P(("groups", "section"), "space", None, None)
    ocean = P(("groups", "section"), "space", None)
    margin = P("space", None, None)
    return jax.shard_map(
        local,
        mesh=mesh,
        in_specs=(state, ocean, margin, margin, margin, P("space", None)) + (P(),) * 12,
        out_specs=(state, ocean),
        check_vma=False,
    )
```

time: 71.6 us -> 41 us (0.57)
  Pallas kernels: 0 us -> 31.8 us
  blocking collectives: 31.6 us -> 0 us
  starting transfers between devices: 16.8 us -> 0 us
  waiting for transfers between devices: 7.92 us -> 0 us
  matrix products: 6.33 us -> 0 us
  local copies, waits for them, and re-layouts: 4.64 us -> 8.27 us
  other arithmetic: 2.53 us -> 0 us
    pallas_call x0 -> x1, Pallas kernels: none -> 31.8 us  [local(): pl.pallas_call(functools.partial(kernel, n, slots), out_shape=(jax.ShapeD...]
    all_gather x1 -> x0, blocking collectives: 21 us -> none  [entering(): gathered = lax.all_gather(part, axis)]
    all_to_all x1 -> x0, blocking collectives: 10.6 us -> none  [local(): lax.all_to_all(send_rows.reshape(peer_count, slot_count, flux_width), 'sp...]
    all_to_all x2 -> x0, starting transfers between devices: 10.5 us -> none  [the longest x1 6.96 us: local(): lax.all_to_all(send_cells.reshape(peer_count, slot_count), 'space', split...]
    all_to_all x2 -> x0, waiting for transfers between devices: 7.92 us -> none  [the longest x1 7.91 us: local(): lax.all_to_all(back_rows.reshape(peer_count, slot_count, flux_width), 'sp...]
    dot_general x10 -> x0, matrix products: 6.33 us -> none  [the longest x1 1.25 us: local(): jnp.dot(cell_onehot, surface, preferred_element_type=jnp.float32)]
    ppermute x2 -> x0, starting transfers between devices: 6.3 us -> none  [the longest x1 5.01 us: extended(): lax.ppermute(tail, axis, [(i, (i + 1) % count) for i in range(ends)])]
    unnamed x41 -> x5, local copies, waits for them, and re-layouts: 2.22 us -> 8.27 us
  transfers between devices with their start and end apart: 4 -> 0, of which waited for: 1 -> 0; matrix products, arithmetic and copies ran while one was open for 13% -> 0% of each run, Pallas kernels for 0% -> 0%
where the time goes in v1:
time: 41 us; the launch traced here: 40.7 us
  Pallas kernels  31.8 us (78%)
  local copies, waits for them, and re-layouts  8.27 us (20%)
  between operations  0.64 us (2%)
    pallas_call x1, Pallas kernels, local(): pl.pallas_call(functools.partial(kernel, n, slots), out_shape=(jax.ShapeD...  31.8 us
    unnamed x5, local copies, waits for them, and re-layouts  8.27 us

profile of v1, /device:TPU:0, one launch (start us, length us, event | category | flops | bytes accessed | tf_op | source)
XLA Modules:
  0.0 40.7 jit_solution(5902149768910950844)
XLA Ops:
  0.6 1.5 %copy.21.forc_hbm = bf16[128,192]{1,0:T(8,128)(2,1)} copy(bf16[128,192]{0,1:T(8,128)(2,1)} %param.30) | data formatting | bytes 98304 | tf_op args[12]
  2.2 1.7 %copy.20 = bf16[1,256,192]{2,1,0:T(8,128)(2,1)} copy(bf16[1,256,192]{1,2,0:T(8,128)(2,1)} %param.19) | data formatting | bytes 196608 | tf_op args[1]
  3.8 1.9 %copy.22.oout_hbm = bf16[768,192]{1,0:T(8,128)(2,1)} copy(bf16[768,192]{0,1:T(8,128)(2,1)} %param.33) | data formatting | bytes 589824 | tf_op args[15]
  5.7 31.8 %shard_map.185 = (bf16[256,256]{1,0:T(8,128)(2,1)}, bf16[256,192]{1,0:T(8,128)(2,1)}) custom-call(bf16[256,256]{1,0:T(8,128)(2,1)} %bitcast.18, s32[2,256]{1,0:T(2,128)} %bitcast.19, s32[2,256]{1,0:T(2,128)} %bitcast.20, f32[2,256]{1,0:T(2,128)} %bitcast.21, s32[1,256]{1,0:T(1,128)} %sea_ref.1, f32[1,256]{1,0:T(1,128)} %bitcast.22, f32[1,192]{1,0:T(1,128)} %bitcast.23, ...), custom_call_target="tpu_custom_call" | custom-call | tf_op jit(solution)/shard_map/pallas_call | solution.py:437
  37.5 1.6 %copy.23 = bf16[1,256,192]{1,2,0:T(8,128)(2,1)} copy(bf16[1,256,192]{2,1,0:T(8,128)(2,1)} %bitcast.16) | data formatting | bytes 196608
  39.1 1.6 %copy.25 = bf16[1,1,256,256]{3,2,1,0:T(8,128)(2,1)} copy(bf16[1,1,256,256]{3,2,1,0:T(8,128)(2,1)} %bitcast.17) | data formatting | bytes 262144

commit v2 on v1

--- a/solution.py
+++ b/solution.py
@@ -57,30 +57,29 @@
     sea_ref,
     again_ref,
     ogain_ref,
-    ocn_hbm,
     conv_hbm,
     mer_hbm,
     ain_hbm,
     aout_hbm,
     flux_hbm,
+    ocn_hbm,
     forc_hbm,
     oin_hbm,
     oout_hbm,
     surf_hbm,
-    feed_hbm,
-    atm_out_ref,
+    back_ref,
+    mid_out_ref,
     ocn_out_ref,
-    ocn_v,
     conv_v,
     mer_v,
     ain_v,
     aout_v,
     flux_v,
+    ocn_v,
     forc_v,
     oin_v,
     oout_v,
     surf_v,
-    feed_v,
     north,
     south,
     sums_send,
@@ -135,7 +134,6 @@
                 (oin_hbm, oin_v),
                 (oout_hbm, oout_v),
                 (surf_hbm, surf_v),
-                (feed_hbm, feed_v),
             ]
         )
     ]
@@ -278,7 +276,7 @@
 
     for copy in cell_copies:
         copy.wait_recv()
-    cells = ocn_v.shape[0]
+    cells = ocn_v.shape[1]
 
     def gather_one(p):
         named = cells_all[p]
@@ -309,7 +307,6 @@
     normed = rms_scale(lifted, again_ref[...]).astype(BF16)
     activated = silu(mm(normed, ain_v[...])).astype(BF16)
     atm_mid = (lifted + mm(activated, aout_v[...])).astype(BF16)
-    mid_v[...] = atm_mid
     flux = mm(atm_mid, flux_v[...]).astype(BF16)
 
     flux_copies = []
@@ -327,6 +324,10 @@
         )
         flux_copies[-1].start()
     recv_rows[me] = mm(pack[me], flux).astype(BF16)
+    mid_v[...] = atm_mid
+    put_mid = pltpu.make_async_copy(mid_v, mid_out_ref, out_sem.at[0])
+    put_mid.start()
+    ocean = jnp.transpose(ocn_v[...].astype(F32))
     for copy in flux_copies:
         copy.wait_recv()
 
@@ -344,10 +345,11 @@
         return lax.fori_loop(0, n // block, term, acc)
 
     forcing = reduced(gather_t, recv_rows).astype(BF16)
-    ocean_lift = ocn_v[...].astype(F32) + mm(forcing, forc_v[...])
+    ocean_lift = ocean + mm_nt(forcing, forc_v[...])
     ocean_normed = rms_scale(ocean_lift, ogain_ref[...]).astype(BF16)
     ocean_act = silu(mm(ocean_normed, oin_v[...])).astype(BF16)
-    ocean_next = (ocean_lift + mm(ocean_act, oout_v[...])).astype(BF16)
+    ocean_new = ocean_lift + mm_nt(ocean_act, oout_v[...])
+    ocean_next = ocean_new.astype(BF16)
     surface = mm(ocean_next, surf_v[...]).astype(BF16)
 
     back_copies = []
@@ -365,9 +367,9 @@
         )
         back_copies[-1].start()
     ret_rows[me] = mm(gather[me], surface).astype(BF16)
-    ocn_new[...] = ocean_next
-    put = pltpu.make_async_copy(ocn_new, ocn_out_ref, out_sem)
-    put.start()
+    ocn_new[...] = jnp.transpose(ocean_new).astype(BF16)
+    put_ocn = pltpu.make_async_copy(ocn_new, ocn_out_ref, out_sem.at[1])
+    put_ocn.start()
 
     for copies in (sum_copies, cell_copies, flux_copies):
         for copy in copies:
@@ -383,11 +385,16 @@
 
     for copy in back_copies:
         copy.wait_recv()
-    feedback = reduced(unpack, ret_rows).astype(BF16)
-    atm_out_ref[...] = (mid_v[...].astype(F32) + mm(feedback, feed_v[...])).astype(BF16)
+    back_ref[...] = reduced(unpack, ret_rows).astype(BF16)
     for copy in back_copies:
         copy.wait_send()
-    put.wait()
+    put_mid.wait()
+    put_ocn.wait()
+
+
+def finish(back_ref, mid_ref, ocn_ref, feed_ref, atm_out_ref, ocn_out_ref):
+    ocn_out_ref[...] = ocn_ref[...]
+    atm_out_ref[...] = (mid_ref[...].astype(F32) + mm(back_ref[...], feed_ref[...])).astype(BF16)
 
 
 def local(
@@ -421,27 +428,27 @@
     vmem = pl.BlockSpec(memory_space=pltpu.VMEM)
     hbm = pl.BlockSpec(memory_space=pl.ANY)
     weights = [
-        ocean_state[0],
         conv_kernel,
         meridional_weight,
         atm_in,
         atm_out,
         flux_weight,
-        forcing_weight,
+        jnp.swapaxes(ocean_state[0], 0, 1),
+        jnp.swapaxes(forcing_weight, 0, 1),
         ocean_in,
-        ocean_out,
+        jnp.swapaxes(ocean_out, 0, 1),
         surface_weight,
-        feedback_weight,
     ]
     dma = lambda count: pltpu.SemaphoreType.DMA((count,))
-    atm_new, ocn_new = pl.pallas_call(
+    back, mid, ocn = pl.pallas_call(
         functools.partial(kernel, n, slots),
         out_shape=(
+            jax.ShapeDtypeStruct((lon, width), BF16),
             jax.ShapeDtypeStruct((lon, channels), BF16),
-            jax.ShapeDtypeStruct((cells, ocn_ch), BF16),
+            jax.ShapeDtypeStruct((ocn_ch, cells), BF16),
         ),
         in_specs=[vmem] * 7 + [hbm] * len(weights),
-        out_specs=(vmem, hbm),
+        out_specs=(vmem, hbm, hbm),
         scratch_shapes=[pltpu.VMEM(w.shape, w.dtype) for w in weights]
         + [
             pltpu.VMEM((lon, channels), BF16),
@@ -459,9 +466,9 @@
             pltpu.VMEM((n, slots, width), BF16),
             pltpu.VMEM((n, slots, width), BF16),
             pltpu.VMEM((lon, channels), BF16),
-            pltpu.VMEM((cells, ocn_ch), BF16),
+            pltpu.VMEM((ocn_ch, cells), BF16),
             dma(len(weights)),
-            pltpu.SemaphoreType.DMA,
+            dma(2),
             dma(2),
             dma(2),
         ]
@@ -479,7 +486,16 @@
         ocean_gain[None, :],
         *weights,
     )
-    return atm_new.reshape(1, lat_rows, lon, channels), ocn_new[None]
+    atm_new, ocn_new = pl.pallas_call(
+        finish,
+        out_shape=(
+            jax.ShapeDtypeStruct((lon, channels), BF16),
+            jax.ShapeDtypeStruct((ocn_ch, cells), BF16),
+        ),
+        in_specs=[vmem] * 4,
+        out_specs=(vmem, vmem),
+    )(back, mid, ocn, feedback_weight)
+    return atm_new.reshape(1, lat_rows, lon, channels), jnp.swapaxes(ocn_new, 0, 1)[None]
 
 
 def solution(mesh):

time: 41 us -> 34.2 us (0.83)
  local copies, waits for them, and re-layouts: 8.27 us -> 0 us
  Pallas kernels: 31.8 us -> 33.4 us
    unnamed x5 -> x0, local copies, waits for them, and re-layouts: 8.27 us -> none
    pallas_call x0 -> x1, Pallas kernels: none -> 1.82 us  [local(): pl.pallas_call(finish, out_shape=(jax.ShapeDtypeStruct((lon, channels), B...]
where the time goes in v2:
time: 34.2 us; the launch traced here: 34.1 us
  Pallas kernels  33.4 us (98%)
  between operations  0.65 us (2%)
    pallas_call x1, Pallas kernels, local(): pl.pallas_call(functools.partial(kernel, n, slots), out_shape=(jax.ShapeD...  31.6 us
    pallas_call x1, Pallas kernels, local(): pl.pallas_call(finish, out_shape=(jax.ShapeDtypeStruct((lon, channels), B...  1.82 us

profile of v2, /device:TPU:0, one launch (start us, length us, event | category | flops | bytes accessed | tf_op | source)
XLA Modules:
  0.0 34.1 jit_solution(9438477105568691320)
XLA Ops:
  0.6 31.6 %shard_map.185 = (bf16[256,128]{1,0:T(8,128)(2,1)}, bf16[256,256]{1,0:T(8,128)(2,1)}, bf16[192,256]{1,0:T(8,128)(2,1)}) custom-call(bf16[256,256]{1,0:T(8,128)(2,1)} %bitcast.22, s32[2,256]{1,0:T(2,128)} %bitcast.25, s32[2,256]{1,0:T(2,128)} %bitcast.26, f32[2,256]{1,0:T(2,128)} %bitcast.27, s32[1,256]{1,0:T(1,128)} %sea_ref.1, f32[1,256]{1,0:T(1,128)} %bitcast.28, ...), custom_call_target="tpu_custom_call" | custom-call | tf_op jit(solution)/shard_map/pallas_call | solution.py:443
  32.3 1.8 %shard_map.186 = (bf16[256,256]{1,0:T(8,128)(2,1)}, bf16[192,256]{1,0:T(8,128)(2,1)}) custom-call(bf16[256,128]{1,0:T(8,128)(2,1)} %get-tuple-element.7.back_ref, bf16[256,256]{1,0:T(8,128)(2,1)} %get-tuple-element.8.mid_ref, bf16[192,256]{1,0:T(8,128)(2,1)} %get-tuple-element.9.ocn_ref, bf16[128,256]{1,0:T(8,128)(2,1)} %feed_ref.1), custom_call_target="tpu_custom_call" | custom-call | tf_op jit(solution)/shard_map/pallas_call | solution.py:489

commit v3 on v2

--- a/solution.py
+++ b/solution.py
@@ -154,6 +154,35 @@
     sums_send[...] = jnp.broadcast_to(total, sums_send.shape)
     sums_all[me] = jnp.broadcast_to(total, sums_send.shape)
 
+    pl.semaphore_wait(barrier, n - 1)
+
+    sum_copies, cell_copies = [], []
+    for d in range(1, n):
+        peer = lax.rem(me + d, n)
+        sum_copies.append(
+            remote(sums_send, sums_all.at[me], sum_send_sem.at[d], sum_recv_sem.at[d], peer)
+        )
+        sum_copies[-1].start()
+
+    up = remote(atm_ref, north, halo_send.at[0], halo_recv.at[0], lax.rem(me + 1, n))
+    down = remote(atm_ref, south, halo_send.at[1], halo_recv.at[1], lax.rem(me + n - 1, n))
+
+    @pl.when(me < n - 1)
+    def _():
+        up.start()
+
+    @pl.when(me > 0)
+    def _():
+        down.start()
+
+    @pl.when(me == 0)
+    def _():
+        north[...] = jnp.zeros_like(north)
+
+    @pl.when(me == n - 1)
+    def _():
+        south[...] = jnp.zeros_like(south)
+
     own_row = jnp.concatenate([own_ref[0:1, :], own_ref[1:2, :]], axis=1)
     entries = own_row.shape[1]
     hits = own_row == lax.broadcasted_iota(jnp.int32, (n, entries), 0)
@@ -182,27 +211,6 @@
     each(n, pack_one)
     cells_all[me] = cells_send[me]
 
-    pl.semaphore_wait(barrier, n - 1)
-
-    up = remote(atm_ref, north, halo_send.at[0], halo_recv.at[0], lax.rem(me + 1, n))
-    down = remote(atm_ref, south, halo_send.at[1], halo_recv.at[1], lax.rem(me + n - 1, n))
-
-    sum_copies, cell_copies = [], []
-    for d in range(1, n):
-        peer = lax.rem(me + d, n)
-        sum_copies.append(
-            remote(sums_send, sums_all.at[me], sum_send_sem.at[d], sum_recv_sem.at[d], peer)
-        )
-        sum_copies[-1].start()
-
-    @pl.when(me < n - 1)
-    def _():
-        up.start()
-
-    @pl.when(me > 0)
-    def _():
-        down.start()
-
     for d in range(1, n):
         peer = lax.rem(me + d, n)
         cell_copies.append(
@@ -215,29 +223,6 @@
             )
         )
         cell_copies[-1].start()
-
-    @pl.when(me == 0)
-    def _():
-        north[...] = jnp.zeros_like(north)
-
-    @pl.when(me == n - 1)
-    def _():
-        south[...] = jnp.zeros_like(south)
-
-    stacked = jnp.concatenate(
-        [slot0, slot1, weight0, weight1, jnp.zeros((4, lon), F32)], axis=0
-    )
-    columns = jnp.transpose(stacked)
-    slot0c, slot1c = columns[:, 0:1], columns[:, 1:2]
-    weight0c, weight1c = columns[:, 2:3], columns[:, 3:4]
-
-    def unpack_one(p):
-        place = (lax.broadcasted_iota(jnp.int32, (lon, slots), 1) + p * slots).astype(F32)
-        unpack[:, pl.ds(p * slots, slots)] = (
-            jnp.where(slot0c == place, weight0c, 0.0) + jnp.where(slot1c == place, weight1c, 0.0)
-        ).astype(BF16)
-
-    each(n, unpack_one)
 
     loads[0].wait()
     centre = atm_ref[...]
@@ -274,21 +259,6 @@
         mm(thirds(jnp.broadcast_to(prefix, (8, channels))), mer_v[...]), axis=0, keepdims=True
     )
 
-    for copy in cell_copies:
-        copy.wait_recv()
-    cells = ocn_v.shape[1]
-
-    def gather_one(p):
-        named = cells_all[p]
-        rows = lax.broadcasted_iota(jnp.int32, (cells, slots), 0).astype(F32)
-        gather_t[:, pl.ds(p * slots, slots)] = jnp.where(named[0:1, :] == rows, 1.0, 0.0).astype(
-            BF16
-        )
-        lanes = lax.broadcasted_iota(jnp.int32, (slots, cells), 1).astype(F32)
-        gather[p] = jnp.where(jnp.transpose(named)[:, 0:1] == lanes, 1.0, 0.0).astype(BF16)
-
-    each(n, gather_one)
-
     for load in loads[2:]:
         load.wait()
 
@@ -328,6 +298,21 @@
     put_mid = pltpu.make_async_copy(mid_v, mid_out_ref, out_sem.at[0])
     put_mid.start()
     ocean = jnp.transpose(ocn_v[...].astype(F32))
+    for copy in cell_copies:
+        copy.wait_recv()
+    cells = ocn_v.shape[1]
+
+    def gather_one(p):
+        named = cells_all[p]
+        rows = lax.broadcasted_iota(jnp.int32, (cells, slots), 0).astype(F32)
+        gather_t[:, pl.ds(p * slots, slots)] = jnp.where(named[0:1, :] == rows, 1.0, 0.0).astype(
+            BF16
+        )
+        lanes = lax.broadcasted_iota(jnp.int32, (slots, cells), 1).astype(F32)
+        gather[p] = jnp.where(jnp.transpose(named)[:, 0:1] == lanes, 1.0, 0.0).astype(BF16)
+
+    each(n, gather_one)
+
     for copy in flux_copies:
         copy.wait_recv()
 
@@ -370,6 +355,21 @@
     ocn_new[...] = jnp.transpose(ocean_new).astype(BF16)
     put_ocn = pltpu.make_async_copy(ocn_new, ocn_out_ref, out_sem.at[1])
     put_ocn.start()
+
+    stacked = jnp.concatenate(
+        [slot0, slot1, weight0, weight1, jnp.zeros((4, lon), F32)], axis=0
+    )
+    columns = jnp.transpose(stacked)
+    slot0c, slot1c = columns[:, 0:1], columns[:, 1:2]
+    weight0c, weight1c = columns[:, 2:3], columns[:, 3:4]
+
+    def unpack_one(p):
+        place = (lax.broadcasted_iota(jnp.int32, (lon, slots), 1) + p * slots).astype(F32)
+        unpack[:, pl.ds(p * slots, slots)] = (
+            jnp.where(slot0c == place, weight0c, 0.0) + jnp.where(slot1c == place, weight1c, 0.0)
+        ).astype(BF16)
+
+    each(n, unpack_one)
 
     for copies in (sum_copies, cell_copies, flux_copies):
         for copy in copies:

time: 34.2 us -> 33.5 us (0.980)
  Pallas kernels: 33.4 us -> 32.7 us
    pallas_call x1, Pallas kernels: 31.6 us -> 30.9 us  [local(): pl.pallas_call(functools.partial(kernel, n, slots), out_shape=(jax.ShapeD...]
where the time goes in v3:
time: 33.5 us; the launch traced here: 33.3 us
  Pallas kernels  32.7 us (98%)
  between operations  0.65 us (2%)
    pallas_call x1, Pallas kernels, local(): pl.pallas_call(functools.partial(kernel, n, slots), out_shape=(jax.ShapeD...  30.9 us
    pallas_call x1, Pallas kernels, local(): pl.pallas_call(finish, out_shape=(jax.ShapeDtypeStruct((lon, channels), B...  1.82 us

profile of v3, /device:TPU:0, one launch (start us, length us, event | category | flops | bytes accessed | tf_op | source)
XLA Modules:
  0.0 33.3 jit_solution(2280081390669984552)
XLA Ops:
  0.6 30.9 %shard_map.185 = (bf16[256,128]{1,0:T(8,128)(2,1)}, bf16[256,256]{1,0:T(8,128)(2,1)}, bf16[192,256]{1,0:T(8,128)(2,1)}) custom-call(bf16[256,256]{1,0:T(8,128)(2,1)} %bitcast.22, s32[2,256]{1,0:T(2,128)} %bitcast.25, s32[2,256]{1,0:T(2,128)} %bitcast.26, f32[2,256]{1,0:T(2,128)} %bitcast.27, s32[1,256]{1,0:T(1,128)} %sea_ref.1, f32[1,256]{1,0:T(1,128)} %bitcast.28, ...), custom_call_target="tpu_custom_call" | custom-call | tf_op jit(solution)/shard_map/pallas_call | solution.py:443
  31.5 1.8 %shard_map.186 = (bf16[256,256]{1,0:T(8,128)(2,1)}, bf16[192,256]{1,0:T(8,128)(2,1)}) custom-call(bf16[256,128]{1,0:T(8,128)(2,1)} %get-tuple-element.7.back_ref, bf16[256,256]{1,0:T(8,128)(2,1)} %get-tuple-element.8.mid_ref, bf16[192,256]{1,0:T(8,128)(2,1)} %get-tuple-element.9.ocn_ref, bf16[128,256]{1,0:T(8,128)(2,1)} %feed_ref.1), custom_call_target="tpu_custom_call" | custom-call | tf_op jit(solution)/shard_map/pallas_call | solution.py:489

commit v4 on v3

--- a/solution.py
+++ b/solution.py
@@ -25,7 +25,8 @@
 
 
 def silu(values):
-    return values / (1.0 + jnp.exp(-values))
+    half = 0.5 * values
+    return half + half * jnp.tanh(half)
 
 
 def thirds(rows):
@@ -151,8 +152,8 @@
         )
 
     total = jnp.sum(atm_ref[...].astype(F32), axis=0, keepdims=True)
-    sums_send[...] = jnp.broadcast_to(total, sums_send.shape)
-    sums_all[me] = jnp.broadcast_to(total, sums_send.shape)
+    sums_send[...] = total
+    sums_all[me] = total
 
     pl.semaphore_wait(barrier, n - 1)
 
@@ -204,9 +205,10 @@
         place = (lax.broadcasted_iota(jnp.int32, (slots, lon), 0) + p * slots).astype(F32)
         hit0, hit1 = slot0 == place, slot1 == place
         pack[p] = (jnp.where(hit0, weight0, 0.0) + jnp.where(hit1, weight1, 0.0)).astype(BF16)
-        cells_send[p] = mm_nt(target0, jnp.where(hit0, 1.0, 0.0).astype(BF16)) + mm_nt(
+        named = mm_nt(target0, jnp.where(hit0, 1.0, 0.0).astype(BF16)) + mm_nt(
             target1, jnp.where(hit1, 1.0, 0.0).astype(BF16)
         )
+        cells_send[p] = named[0:1, :]
 
     each(n, pack_one)
     cells_all[me] = cells_send[me]
@@ -230,7 +232,7 @@
 
     for copy in sum_copies:
         copy.wait_recv()
-    zeros = jnp.zeros((8, channels), F32)
+    zeros = jnp.zeros((1, channels), F32)
 
     def tally(p, sums):
         before, through, after = sums
@@ -248,10 +250,10 @@
         carried = lax.fori_loop(0, n, tally, (zeros, zeros, zeros))
     mixed = jnp.zeros((8, channels), F32)
     for a in range(3):
-        parts = thirds(carried[a])
+        parts = thirds(jnp.broadcast_to(carried[a], (8, channels)))
         for b in range(3):
             mixed = mixed + mm(parts, conv_v[3 * a + b])
-    prefix = (carried[1][0:1, :] + jnp.sum(mixed, axis=0, keepdims=True)) * (
+    prefix = (carried[1] + jnp.sum(mixed, axis=0, keepdims=True)) * (
         1.0 / (math.sqrt(lon) * math.sqrt(n))
     )
     loads[1].wait()
@@ -303,7 +305,7 @@
     cells = ocn_v.shape[1]
 
     def gather_one(p):
-        named = cells_all[p]
+        named = jnp.broadcast_to(cells_all[p], (8, slots))
         rows = lax.broadcasted_iota(jnp.int32, (cells, slots), 0).astype(F32)
         gather_t[:, pl.ds(p * slots, slots)] = jnp.where(named[0:1, :] == rows, 1.0, 0.0).astype(
             BF16
@@ -453,10 +455,10 @@
         + [
             pltpu.VMEM((lon, channels), BF16),
             pltpu.VMEM((lon, channels), BF16),
-            pltpu.VMEM((8, channels), F32),
-            pltpu.VMEM((n, 8, channels), F32),
-            pltpu.VMEM((n, 8, slots), F32),
-            pltpu.VMEM((n, 8, slots), F32),
+            pltpu.VMEM((1, channels), F32),
+            pltpu.VMEM((n, 1, channels), F32),
+            pltpu.VMEM((n, 1, slots), F32),
+            pltpu.VMEM((n, 1, slots), F32),
             pltpu.VMEM((n, slots, lon), BF16),
             pltpu.VMEM((lon, n * slots), BF16),
             pltpu.VMEM((cells, n * slots), BF16),

time: 33.5 us -> 32.9 us (0.982)
  Pallas kernels: 32.7 us -> 32.1 us
    pallas_call x1, Pallas kernels: 30.9 us -> 30.3 us  [local(): pl.pallas_call(functools.partial(kernel, n, slots), out_shape=(jax.ShapeD...]
where the time goes in v4:
time: 32.9 us; the launch traced here: 32.8 us
  Pallas kernels  32.1 us (98%)
  between operations  0.65 us (2%)
    pallas_call x1, Pallas kernels, local(): pl.pallas_call(functools.partial(kernel, n, slots), out_shape=(jax.ShapeD...  30.3 us
    pallas_call x1, Pallas kernels, local(): pl.pallas_call(finish, out_shape=(jax.ShapeDtypeStruct((lon, channels), B...  1.83 us

profile of v4, /device:TPU:0, one launch (start us, length us, event | category | flops | bytes accessed | tf_op | source)
XLA Modules:
  0.0 32.8 jit_solution(8491296890640174491)
XLA Ops:
  0.6 30.3 %shard_map.185 = (bf16[256,128]{1,0:T(8,128)(2,1)}, bf16[256,256]{1,0:T(8,128)(2,1)}, bf16[192,256]{1,0:T(8,128)(2,1)}) custom-call(bf16[256,256]{1,0:T(8,128)(2,1)} %bitcast.22, s32[2,256]{1,0:T(2,128)} %bitcast.25, s32[2,256]{1,0:T(2,128)} %bitcast.26, f32[2,256]{1,0:T(2,128)} %bitcast.27, s32[1,256]{1,0:T(1,128)} %sea_ref.1, f32[1,256]{1,0:T(1,128)} %bitcast.28, ...), custom_call_target="tpu_custom_call" | custom-call | tf_op jit(solution)/shard_map/pallas_call | solution.py:445
  30.9 1.8 %shard_map.186 = (bf16[256,256]{1,0:T(8,128)(2,1)}, bf16[192,256]{1,0:T(8,128)(2,1)}) custom-call(bf16[256,128]{1,0:T(8,128)(2,1)} %get-tuple-element.7.back_ref, bf16[256,256]{1,0:T(8,128)(2,1)} %get-tuple-element.8.mid_ref, bf16[192,256]{1,0:T(8,128)(2,1)} %get-tuple-element.9.ocn_ref, bf16[128,256]{1,0:T(8,128)(2,1)} %feed_ref.1), custom_call_target="tpu_custom_call" | custom-call | tf_op jit(solution)/shard_map/pallas_call | solution.py:491

commit v5 on v4

--- a/solution.py
+++ b/solution.py
@@ -268,12 +268,15 @@
     def _():
         up.wait_recv()
 
+    above = north[...]
+    taps = [taps[b] + mm(above, conv_v[b]) for b in range(3)]
+
     @pl.when(me < n - 1)
     def _():
         down.wait_recv()
 
-    above, below = north[...], south[...]
-    taps = [taps[b] + mm(above, conv_v[b]) + mm(below, conv_v[6 + b]) for b in range(3)]
+    below = south[...]
+    taps = [taps[b] + mm(below, conv_v[6 + b]) for b in range(3)]
     mixing = pltpu.roll(taps[0], 1, 0) + taps[1] + pltpu.roll(taps[2], lon - 1, 0)
     lifted = atm_ref[...].astype(F32) + mixing + meridional
     normed = rms_scale(lifted, again_ref[...]).astype(BF16)
@@ -315,23 +318,19 @@
 
     each(n, gather_one)
 
-    for copy in flux_copies:
-        copy.wait_recv()
-
     width = flux.shape[1]
-    block = math.gcd(n, 8)
-
-    def reduced(matrix, rows):
-        def term(q, acc):
-            part = rows[pl.ds(q * block, block)].reshape(block * slots, width)
-            return acc + mm(matrix[:, pl.ds(q * block * slots, block * slots)], part)
-
+
+    def reduced(matrix, rows, copies):
         acc = jnp.zeros((matrix.shape[0], width), F32)
-        if n == block:
-            return term(0, acc)
-        return lax.fori_loop(0, n // block, term, acc)
-
-    forcing = reduced(gather_t, recv_rows).astype(BF16)
+        for d in range(n):
+            if d > 0:
+                copies[d - 1].wait_recv()
+            source = lax.rem(me + n - d, n)
+            lanes = pl.ds(pl.multiple_of(source * slots, 128), slots)
+            acc = acc + mm(matrix[:, lanes], rows[source])
+        return acc
+
+    forcing = reduced(gather_t, recv_rows, flux_copies).astype(BF16)
     ocean_lift = ocean + mm_nt(forcing, forc_v[...])
     ocean_normed = rms_scale(ocean_lift, ogain_ref[...]).astype(BF16)
     ocean_act = silu(mm(ocean_normed, oin_v[...])).astype(BF16)
@@ -385,9 +384,7 @@
     def _():
         down.wait_send()
 
-    for copy in back_copies:
-        copy.wait_recv()
-    back_ref[...] = reduced(unpack, ret_rows).astype(BF16)
+    back_ref[...] = reduced(unpack, ret_rows, back_copies).astype(BF16)
     for copy in back_copies:
         copy.wait_send()
     put_mid.wait()

time: 32.9 us -> 33.4 us (1.015)
  Pallas kernels: 32.1 us -> 32.6 us
    pallas_call x1, Pallas kernels: 30.3 us -> 30.8 us  [local(): pl.pallas_call(functools.partial(kernel, n, slots), out_shape=(jax.ShapeD...]
where the time goes in v5:
time: 33.4 us; the launch traced here: 33.3 us
  Pallas kernels  32.6 us (98%)
  between operations  0.65 us (2%)
    pallas_call x1, Pallas kernels, local(): pl.pallas_call(functools.partial(kernel, n, slots), out_shape=(jax.ShapeD...  30.8 us
    pallas_call x1, Pallas kernels, local(): pl.pallas_call(finish, out_shape=(jax.ShapeDtypeStruct((lon, channels), B...  1.82 us

profile of v5, /device:TPU:0, one launch (start us, length us, event | category | flops | bytes accessed | tf_op | source)
XLA Modules:
  0.0 33.3 jit_solution(12189876008425835757)
XLA Ops:
  0.6 30.8 %shard_map.185 = (bf16[256,128]{1,0:T(8,128)(2,1)}, bf16[256,256]{1,0:T(8,128)(2,1)}, bf16[192,256]{1,0:T(8,128)(2,1)}) custom-call(bf16[256,256]{1,0:T(8,128)(2,1)} %bitcast.22, s32[2,256]{1,0:T(2,128)} %bitcast.25, s32[2,256]{1,0:T(2,128)} %bitcast.26, f32[2,256]{1,0:T(2,128)} %bitcast.27, s32[1,256]{1,0:T(1,128)} %sea_ref.1, f32[1,256]{1,0:T(1,128)} %bitcast.28, ...), custom_call_target="tpu_custom_call" | custom-call | tf_op jit(solution)/shard_map/pallas_call | solution.py:442
  31.4 1.8 %shard_map.186 = (bf16[256,256]{1,0:T(8,128)(2,1)}, bf16[192,256]{1,0:T(8,128)(2,1)}) custom-call(bf16[256,128]{1,0:T(8,128)(2,1)} %get-tuple-element.7.back_ref, bf16[256,256]{1,0:T(8,128)(2,1)} %get-tuple-element.8.mid_ref, bf16[192,256]{1,0:T(8,128)(2,1)} %get-tuple-element.9.ocn_ref, bf16[128,256]{1,0:T(8,128)(2,1)} %feed_ref.1), custom_call_target="tpu_custom_call" | custom-call | tf_op jit(solution)/shard_map/pallas_call | solution.py:488
